TPU v7x, 32 devices: a whole 2x2x4 slice. The times are simulated.
32 devices in a mesh: dp: 8 (over z, y), tensor: 4 (over x, core).
Axes of the slice: x: 2, y: 2, z: 4, core: 2. Of those that a mesh axis runs over, the one named last changes fastest.
Arguments:
- frames: bfloat16 [8, 1024, 768], P('dp'), may hold values from -6 to 6
- frame_mask: int32 [8, 1024], P('dp'), may hold values from 0 to 1, as said below
- mask_embedding: float32 [768], replicated, may hold values from -6 to 6
- query_weight: bfloat16 [768, 768], P(None, 'tensor'), may hold values from -0.21875 to 0.21875
- query_bias: float32 [768], P('tensor'), may hold values from -3 to 3
- key_weight: bfloat16 [768, 768], P(None, 'tensor'), may hold values from -0.21875 to 0.21875
- value_weight: bfloat16 [768, 768], P(None, 'tensor'), may hold values from -0.21875 to 0.21875
- value_bias: float32 [768], P('tensor'), may hold values from -3 to 3
- out_weight: bfloat16 [768, 768], P('tensor'), may hold values from -0.625 to 0.625
- out_bias: float32 [768], replicated, may hold values from -3 to 3
- norm1_gain: float32 [768], replicated, may hold values from 0.5 to 1.5
- norm1_shift: float32 [768], replicated, may hold values from -3 to 3
- up_weight: bfloat16 [768, 3072], P(None, 'tensor'), may hold values from -0.21875 to 0.21875
- up_bias: float32 [3072], P('tensor'), may hold values from -3 to 3
- down_weight: bfloat16 [3072, 768], P('tensor'), may hold values from -0.109375 to 0.109375
- down_bias: float32 [768], replicated, may hold values from -3 to 3
- norm2_gain: float32 [768], replicated, may hold values from 0.5 to 1.5
- norm2_shift: float32 [768], replicated, may hold values from -3 to 3
- cotangent: bfloat16 [8, 1024, 768], P('dp'), may hold values from -6 to 6
Outputs:
- output: bfloat16 [8, 1024, 768], P('dp')
- frames_grad: bfloat16 [8, 1024, 768], P('dp')
- mask_embedding_grad: float32 [768], replicated
- query_weight_grad: float32 [768, 768], P(None, 'tensor')
- query_bias_grad: float32 [768], P('tensor')
- key_weight_grad: float32 [768, 768], P(None, 'tensor')
- value_weight_grad: float32 [768, 768], P(None, 'tensor')
- value_bias_grad: float32 [768], P('tensor')
- out_weight_grad: float32 [768, 768], P('tensor')
- out_bias_grad: float32 [768], replicated
- norm1_gain_grad: float32 [768], replicated
- norm1_shift_grad: float32 [768], replicated
- up_weight_grad: float32 [768, 3072], P(None, 'tensor')
- up_bias_grad: float32 [3072], P('tensor')
- down_weight_grad: float32 [3072, 768], P('tensor')
- down_bias_grad: float32 [768], replicated
- norm2_gain_grad: float32 [768], replicated
- norm2_shift_grad: float32 [768], replicated
Inputs may be any that keep to these rules, and one draw needn't show every extreme that they name: `frame_mask`: 1 marks a frame inside one of 68 spans of 10 frames whose starts are drawn for each clip; spans may intersect.
All inputs are finite; a program needn't handle non-finite values.
Results may differ from a plain program's by a relative error of at most 0.017.
Values sent between devices are 32-bit elements; how exact they have to be, the bound alone decides.
No kernel may reach another device: no remote copies, remote signals or barrier semaphores. Data moves between devices by JAX's collectives and lax.ppermute only.
A program may use at most 128 MiB of HBM per device.

v0:
```python
import math

import jax
import jax.numpy as jnp
from jax import lax
from jax.sharding import PartitionSpec as P

HEAD = 64


def local_dot(left, right):
    return jnp.dot(left, right, preferred_element_type=jnp.float32)


def dot_rows(left, right):
    return lax.dot_general(
        left, right, (((0,), (0,)), ((), ())), preferred_element_type=jnp.float32
    )


def dot_trans(left, right):
    return lax.dot_general(
        left, right, (((1,), (1,)), ((), ())), preferred_element_type=jnp.float32
    )


def normalize(values):
    centered = values - jnp.mean(values, -1, keepdims=True)
    inverse = lax.rsqrt(jnp.mean(centered * centered, -1, keepdims=True) + 1e-05)
    return (centered * inverse, inverse)


def norm_backward(grad_normed, normed, inverse):
    return inverse * (
        grad_normed
        - jnp.mean(grad_normed, -1, keepdims=True)
        - normed * jnp.mean(grad_normed * normed, -1, keepdims=True)
    )


def shards(
    frames,
    frame_mask,
    mask_embedding,
    query_weight,
    query_bias,
    key_weight,
    value_weight,
    value_bias,
    out_weight,
    out_bias,
    norm1_gain,
    norm1_shift,
    up_weight,
    up_bias,
    down_weight,
    down_bias,
    norm2_gain,
    norm2_shift,
    cotangent,
):
    clip_count, length, model_width = frames.shape
    token_rows = clip_count * length
    local_width = query_weight.shape[1]
    heads_here = local_width // HEAD
    score_scale = 1.0 / math.sqrt(HEAD)
    head_shape = (clip_count, length, heads_here, HEAD)
    masked_rows = frame_mask.reshape(token_rows, 1).astype(jnp.float32)
    masked_in = (
        frames.reshape(token_rows, model_width).astype(jnp.float32) * (1.0 - masked_rows)
        + masked_rows * mask_embedding
    )
    masked_low = masked_in.astype(jnp.bfloat16)
    query = (local_dot(masked_low, query_weight) + query_bias).astype(jnp.bfloat16)
    keys = local_dot(masked_low, key_weight).astype(jnp.bfloat16)
    values = (local_dot(masked_low, value_weight) + value_bias).astype(jnp.bfloat16)
    query_heads = query.reshape(head_shape)
    key_heads = keys.reshape(head_shape)
    value_heads = values.reshape(head_shape)
    scores = (
        jnp.einsum("cqhd,ckhd->chqk", query_heads, key_heads, preferred_element_type=jnp.float32)
        * score_scale
    )
    row_max = jnp.max(scores, -1, keepdims=True)
    expo = jnp.exp(scores - row_max)
    totals = jnp.sum(expo, -1, keepdims=True)
    log_sum = row_max + jnp.log(totals)
    attn_low = (expo / totals).astype(jnp.bfloat16)
    context = jnp.einsum(
        "chqk,ckhd->cqhd", attn_low, value_heads, preferred_element_type=jnp.float32
    )
    context = context.reshape(token_rows, local_width).astype(jnp.bfloat16)
    attended = lax.psum(local_dot(context, out_weight), "tensor")
    normed_one, inverse_one = normalize(masked_in + attended + out_bias)
    hidden_one = normed_one * norm1_gain + norm1_shift
    ffn_in = hidden_one.astype(jnp.bfloat16)
    pre_act = local_dot(ffn_in, up_weight) + up_bias
    activ = jax.nn.gelu(pre_act, approximate=False).astype(jnp.bfloat16)
    ffn_out = lax.psum(local_dot(activ, down_weight), "tensor")
    normed_two, inverse_two = normalize(hidden_one + ffn_out + down_bias)
    output = normed_two * norm2_gain + norm2_shift
    grad_out = cotangent.reshape(token_rows, model_width).astype(jnp.float32)
    norm2_gain_grad = jnp.sum(grad_out * normed_two, 0)
    norm2_shift_grad = jnp.sum(grad_out, 0)
    grad_h2 = norm_backward(grad_out * norm2_gain, normed_two, inverse_two)
    down_bias_grad = jnp.sum(grad_h2, 0)
    grad_h2_low = grad_h2.astype(jnp.bfloat16)
    down_weight_grad = dot_rows(activ, grad_h2_low)
    grad_act = dot_trans(grad_h2_low, down_weight)
    normal_cdf = 0.5 * (1.0 + lax.erf(pre_act / math.sqrt(2.0)))
    normal_pdf = jnp.exp(-0.5 * pre_act * pre_act) / math.sqrt(2.0 * math.pi)
    grad_pre = (grad_act * (normal_cdf + pre_act * normal_pdf)).astype(jnp.bfloat16)
    up_bias_grad = jnp.sum(grad_pre.astype(jnp.float32), 0)
    up_weight_grad = dot_rows(ffn_in, grad_pre)
    grad_one = grad_h2 + lax.psum(dot_trans(grad_pre, up_weight), "tensor")
    norm1_gain_grad = jnp.sum(grad_one * normed_one, 0)
    norm1_shift_grad = jnp.sum(grad_one, 0)
    grad_h1 = norm_backward(grad_one * norm1_gain, normed_one, inverse_one)
    out_bias_grad = jnp.sum(grad_h1, 0)
    grad_h1_low = grad_h1.astype(jnp.bfloat16)
    out_weight_grad = dot_rows(context, grad_h1_low)
    grad_context = dot_trans(grad_h1_low, out_weight).astype(jnp.bfloat16).reshape(head_shape)
    scores_again = (
        jnp.einsum("cqhd,ckhd->chqk", query_heads, key_heads, preferred_element_type=jnp.float32)
        * score_scale
    )
    attn_again = jnp.exp(scores_again - log_sum)
    attn_again_low = attn_again.astype(jnp.bfloat16)
    grad_values = jnp.einsum(
        "chqk,cqhd->ckhd", attn_again_low, grad_context, preferred_element_type=jnp.float32
    )
    grad_values = grad_values.astype(jnp.bfloat16).reshape(token_rows, local_width)
    grad_attn = jnp.einsum(
        "cqhd,ckhd->chqk", grad_context, value_heads, preferred_element_type=jnp.float32
    )
    grad_scores = (
        attn_again * (grad_attn - jnp.sum(attn_again * grad_attn, -1, keepdims=True))
    ).astype(jnp.bfloat16)
    grad_query = (
        jnp.einsum("chqk,ckhd->cqhd", grad_scores, key_heads, preferred_element_type=jnp.float32)
        * score_scale
    )
    grad_query = grad_query.astype(jnp.bfloat16).reshape(token_rows, local_width)
    grad_keys = (
        jnp.einsum("chqk,cqhd->ckhd", grad_scores, query_heads, preferred_element_type=jnp.float32)
        * score_scale
    )
    grad_keys = grad_keys.astype(jnp.bfloat16).reshape(token_rows, local_width)
    query_weight_grad = dot_rows(masked_low, grad_query)
    key_weight_grad = dot_rows(masked_low, grad_keys)
    value_weight_grad = dot_rows(masked_low, grad_values)
    query_bias_grad = jnp.sum(grad_query.astype(jnp.float32), 0)
    value_bias_grad = jnp.sum(grad_values.astype(jnp.float32), 0)
    input_terms = (
        dot_trans(grad_query, query_weight)
        + dot_trans(grad_keys, key_weight)
        + dot_trans(grad_values, value_weight)
    )
    grad_in = grad_h1 + lax.psum(input_terms, "tensor")
    frames_grad = (grad_in * (1.0 - masked_rows)).astype(jnp.bfloat16).reshape(frames.shape)
    mask_embedding_grad = jnp.sum(grad_in * masked_rows, 0)
    (
        mask_embedding_grad,
        query_weight_grad,
        query_bias_grad,
        key_weight_grad,
        value_weight_grad,
        value_bias_grad,
        out_weight_grad,
        out_bias_grad,
        norm1_gain_grad,
        norm1_shift_grad,
        up_weight_grad,
        up_bias_grad,
        down_weight_grad,
        down_bias_grad,
        norm2_gain_grad,
        norm2_shift_grad,
    ) = lax.psum(
        (
            mask_embedding_grad,
            query_weight_grad,
            query_bias_grad,
            key_weight_grad,
            value_weight_grad,
            value_bias_grad,
            out_weight_grad,
            out_bias_grad,
            norm1_gain_grad,
            norm1_shift_grad,
            up_weight_grad,
            up_bias_grad,
            down_weight_grad,
            down_bias_grad,
            norm2_gain_grad,
            norm2_shift_grad,
        ),
        "dp",
    )
    return (
        output.astype(jnp.bfloat16).reshape(frames.shape),
        frames_grad,
        mask_embedding_grad,
        query_weight_grad,
        query_bias_grad,
        key_weight_grad,
        value_weight_grad,
        value_bias_grad,
        out_weight_grad,
        out_bias_grad,
        norm1_gain_grad,
        norm1_shift_grad,
        up_weight_grad,
        up_bias_grad,
        down_weight_grad,
        down_bias_grad,
        norm2_gain_grad,
        norm2_shift_grad,
    )


def solution(mesh):
    placed = (
        P("dp", None, None),
        P("dp", None),
        P(),
        P(None, "tensor"),
        P("tensor"),
        P(None, "tensor"),
        P(None, "tensor"),
        P("tensor"),
        P("tensor", None),
        P(),
        P(),
        P(),
        P(None, "tensor"),
        P("tensor"),
        P("tensor", None),
        P(),
        P(),
        P(),
        P("dp", None, None),
    )
    return jax.shard_map(
        shards,
        mesh=mesh,
        in_specs=placed,
        out_specs=(
            P("dp", None, None),
            P("dp", None, None),
            P(),
            P(None, "tensor"),
            P("tensor"),
            P(None, "tensor"),
            P(None, "tensor"),
            P("tensor"),
            P("tensor", None),
            P(),
            P(),
            P(),
            P(None, "tensor"),
            P("tensor"),
            P("tensor", None),
            P(),
            P(),
            P(),
        ),
        check_vma=False,
    )
```

profile of v0, /device:TPU:0, one launch (start us, length us, event | category | flops | bytes accessed | tf_op | source)
XLA Modules:
  0.0 629.2 jit_solution(1069542277354921530)
XLA Ops:
  8.1 1.9 fusion.33
  12.1 1.9 multiply_reduce_fusion.1
  14.0 2.1 fusion
  16.1 2.4 copy-done.2
  18.7 2.6 fusion.46
  22.2 2.3 fusion.63
  24.7 71.0 %all-reduce.8.cloned.1.call-done = f32[1024,768]{1,0:T(8,128)} async-done(((f32[1024,768]{1,0:T(8,128)}), f32[1024,768]{1,0:T(8,128)}) %all-reduce.8.cloned.1.call-update) | async-done | bytes 3145744 | tf_op jit(solution)/shard_map/psum | solution.py:93
  95.8 3.0 fusion.59
  99.6 9.3 %fusion.20 = (bf16[1024,768]{1,0:T(8,128)(2,1)S(1)}, f32[1024,768]{1,0:T(8,128)}) fusion(f32[768]{0:T(1024)S(1)} %copy-done.46, bf16[768,768]{1,0:T(8,128)(2,1)S(1)} %copy-done, f32[1024,768]{1,0:T(8,128)S(1)} %get-tuple-element.49, f32[768]{0:T(1024)S(1)} %copy-done.42, f32[768]{0:T(1024)S(1)} %copy-done.32, f32[1024]{0:T(1024)S(1)} %add_rsqrt_fusion.1, ...), kind=kOutput, calls=%fused_computation.31 | convolution fusion | flops 1263796224 | bytes 9061376 | tf_op jit(solution)/shard_map/dot_general | solution.py:12
  108.9 1.2 copy-done.49
  110.2 3.1 fusion.64
  113.3 68.6 %all-reduce.10.cloned.1.call-done = f32[1024,768]{1,0:T(8,128)} async-done(((f32[1024,768]{1,0:T(8,128)}), f32[1024,768]{1,0:T(8,128)}) %all-reduce.10.cloned.1.call-update) | async-done | bytes 3145744 | tf_op jit(solution)/shard_map/psum | solution.py:99
  181.9 3.9 fusion.58
  186.4 0.8 copy-done.9
  187.2 2.0 fusion.13
  189.2 2.9 fusion.56
  192.1 2.9 convert_reduce_fusion.1
  195.1 1.1 copy-done.50
  196.2 3.1 fusion.65
  200.1 1.9 fusion.38
  202.0 5.5 fusion.60
  207.6 60.5 %all-reduce.12.cloned.1.call-done = f32[1024,768]{1,0:T(8,128)} async-done(((f32[1024,768]{1,0:T(8,128)}), f32[1024,768]{1,0:T(8,128)}) %all-reduce.12.cloned.1.call-update) | async-done | bytes 3145744 | tf_op jit(solution)/shard_map/psum | solution.py:115
  268.0 5.4 multiply_reduce_fusion.2
  273.5 1.0 subtract_multiply_fusion
  274.5 1.6 copy-done.6
  276.9 0.9 slice-done.2
  277.8 2.6 convert_reduce_fusion.2
  280.4 4.0 multiply_reduce_fusion
  284.4 5.3 multiply_convert_fusion
  289.7 5.0 fusion.42
  294.7 1.3 convert_reduce_fusion.3
  297.6 2.3 add_add_fusion
  300.3 5.2 fusion.50
  305.5 1.3 fusion.70
  306.8 1.3 fusion.68
  308.1 1.3 fusion.69
  309.4 1.3 fusion.47
  310.7 1.4 copy-done.10
  312.6 56.1 %all-reduce.14.cloned.1.call-done = f32[1024,768]{1,0:T(8,128)} async-done(((f32[1024,768]{1,0:T(8,128)}), f32[1024,768]{1,0:T(8,128)}) %all-reduce.14.cloned.1.call-update) | async-done | bytes 3145744 | tf_op jit(solution)/shard_map/psum | solution.py:159
  368.7 4.6 fusion.55
  373.3 40.1 %all-reduce = (f32[768]{0:T(1024)}, f32[192]{0:T(256)}, f32[192]{0:T(256)}, f32[768]{0:T(1024)}, f32[768]{0:T(1024)}, /*index=5*/f32[768]{0:T(1024)}, f32[768]{0...) all-reduce(f32[768]{0:T(1024)S(1)} %get-tuple-element.25, ...), channel_id=1, replica_groups=mesh['dp'=8,'tensor'=4] {'dp'}, use_global_device_ids=true, to_apply=%region_16.0 | all-reduce | flops 6528 | bytes 52224 | tf_op jit(solution)/shard_map/psum | solution.py:179
  413.4 199.7 %all-reduce.16.cloned.1.call-done = (f32[768,192]{0,1:T(8,128)}, f32[768,192]{0,1:T(8,128)}, f32[768,192]{0,1:T(8,128)}, f32[192,768]{1,0:T(8,128)}, f32[768,768]{1,0:T(8,128)}, /*index=5*/f32[768,768]{1,0:T(8,128)}) async-done(((f32[768,192]{0,1:T(8,128)}, f32[768,192]{0,1:T(8,128)}, f32[768,192]{0,1:T(8,128)}, f32[192,768]{1,0:T(8,128)}, f32[768,768]{1,0:T(8,128)}, /*index=5*/f32[768,768]{1,0:T(8,128)}), ...) | async-done | bytes 7077904 | tf_op jit(solution)/shard_map/psum | solution.py:179
  613.1 2.1 copy.55
  615.2 1.9 copy.56
  617.1 1.9 copy.57
  619.0 0.8 copy.58
  619.9 1.4 copy.59
  621.3 1.4 copy.60
  (135 shorter events, 9.3 us)
Async XLA Ops:
  7.2 92.2 %copy-start = (bf16[768,768]{1,0:T(8,128)(2,1)S(1)}, bf16[768,768]{1,0:T(8,128)(2,1)}, u32[]{:S(2)}) copy-start(bf16[768,768]{1,0:T(8,128)(2,1)} %param.31) | copy-start | bytes 3538948
  7.2 2.8 copy-start.22
  7.2 3.5 copy-start.24
  7.2 3.5 copy-start.47
  7.2 88.5 %all-reduce.8.cloned.1.call-start = ((), (), s32[]{:S(2)}) async-start(), calls=%async_computation | async-start | bytes 6291456 | tf_op jit(solution)/shard_map/psum | solution.py:93
  10.0 1.4 copy-start.20
  12.1 4.0 copy-start.18
  14.0 4.5 copy-start.2
  14.0 4.7 copy-start.26
  16.1 5.3 copy-start.28
  18.7 3.4 copy-start.16
  22.2 73.6 %copy-start.8 = (bf16[1,1024,768]{2,1,0:T(8,128)(2,1)S(1)}, bf16[1,1024,768]{2,1,0:T(8,128)(2,1)}, u32[]{:S(2)}) copy-start(bf16[1,1024,768]{2,1,0:T(8,128)(2,1)} %param.19) | copy-start | bytes 4718596
  22.2 73.6 %copy-start.30 = (f32[768]{0:T(1024)S(1)}, f32[768]{0:T(1024)}, u32[]{:S(2)}) copy-start(f32[768]{0:T(1024)} %param.21) | copy-start | bytes 9220
  22.2 73.6 %copy-start.39 = (f32[768]{0:T(1024)S(1)}, f32[768]{0:T(1024)}, u32[]{:S(2)}) copy-start(f32[768]{0:T(1024)} %param.28) | copy-start | bytes 9220
  24.5 157.5 %all-reduce.10.cloned.1.call-start = ((), (), s32[]{:S(2)}) async-start(), calls=%async_computation.1 | async-start | bytes 6291456 | tf_op jit(solution)/shard_map/psum | solution.py:99
  98.8 10.1 %copy-start.3 = (f32[1024,768]{1,0:T(8,128)}, f32[1024,768]{1,0:T(8,128)S(1)}, u32[]{:S(2)}) copy-start(f32[1024,768]{1,0:T(8,128)S(1)} %get-tuple-element.49) | copy-start | bytes 9437188
  99.6 10.5 %copy-start.45 = (bf16[768,768]{1,0:T(8,128)(2,1)S(1)}, bf16[768,768]{1,0:T(8,128)(2,1)}, u32[]{:S(2)}) copy-start(bf16[768,768]{1,0:T(8,128)(2,1)} %param.33) | copy-start | bytes 3538948
  113.2 68.7 %copy-start.41 = (f32[768]{0:T(1024)S(1)}, f32[768]{0:T(1024)}, u32[]{:S(2)}) copy-start(f32[768]{0:T(1024)} %param.34) | copy-start | bytes 9220
  113.2 154.8 %all-reduce.12.cloned.1.call-start = ((), (), s32[]{:S(2)}) async-start(), calls=%async_computation.2 | async-start | bytes 6291456 | tf_op jit(solution)/shard_map/psum | solution.py:115
  185.8 1.4 copy-start.9
  185.8 1.4 copy-start.34
  186.4 2.8 copy-start.40
  189.2 2.9 copy-start.51
  192.1 2.9 copy-start.11
  199.3 2.7 copy-start.33
  199.3 2.7 copy-start.43
  199.3 169.3 %all-reduce.14.cloned.1.call-start = ((), (), s32[]{:S(2)}) async-start(), calls=%async_computation.3 | async-start | bytes 6291456 | tf_op jit(solution)/shard_map/psum | solution.py:159
  268.0 5.4 copy-start.4
  268.0 8.8 %slice-start = ((s8[12582912]{0:T(1024)(128)(4,1)}), s8[4194304]{0:T(1024)(128)(4,1)S(1)}, s32[]{:S(2)}) async-start(s8[12582912]{0:T(1024)(128)(4,1)} %bitcast.105), calls=%async_computation.5 | async-start | bytes 8388608
  268.0 8.8 %slice-start.1 = ((s8[12582912]{0:T(1024)(128)(4,1)}), s8[4194304]{0:T(1024)(128)(4,1)S(1)}, s32[]{:S(2)}) async-start(s8[12582912]{0:T(1024)(128)(4,1)} %bitcast.105), calls=%async_computation.6 | async-start | bytes 8388608
  273.5 2.7 copy-start.17
  273.5 4.3 slice-start.2
  274.5 1.6 copy-start.6
  289.7 5.0 copy-start.5
  296.0 1.6 copy-start.21
  299.9 313.2 %all-reduce.16.cloned.1.call-start = ((), (), s32[]{:S(2)}) async-start(), calls=%async_computation.4 | async-start | bytes 14155776 | tf_op jit(solution)/shard_map/psum | solution.py:179
  306.8 2.6 copy-start.7
  306.8 2.6 copy-start.15
  310.7 1.4 copy-start.10
  312.5 60.7 %copy-start.35 = (f32[768]{0:T(1024)S(1)}, f32[768]{0:T(1024)}, u32[]{:S(2)}) copy-start(f32[768]{0:T(1024)} %get-tuple-element.43) | copy-start | bytes 9220
  312.6 60.7 %copy-start.36 = (f32[768]{0:T(1024)S(1)}, f32[768]{0:T(1024)}, u32[]{:S(2)}) copy-start(f32[768]{0:T(1024)} %get-tuple-element.18) | copy-start | bytes 9220
  312.6 60.7 %copy-start.37 = (f32[768]{0:T(1024)S(1)}, f32[768]{0:T(1024)}, u32[]{:S(2)}) copy-start(f32[768]{0:T(1024)} %get-tuple-element.23) | copy-start | bytes 9220
  312.6 60.7 %copy-start.38 = (f32[768]{0:T(1024)S(1)}, f32[768]{0:T(1024)}, u32[]{:S(2)}) copy-start(f32[768]{0:T(1024)} %get-tuple-element.20) | copy-start | bytes 9220
  312.6 60.7 %copy-start.44 = (f32[768]{0:T(1024)S(1)}, f32[768]{0:T(1024)}, u32[]{:S(2)}) copy-start(f32[768]{0:T(1024)} %get-tuple-element.62) | copy-start | bytes 9220
  613.1 5.9 copy-start.19
  613.1 6.7 %copy-start.13 = (f32[768,768]{1,0:T(8,128)S(1)}, f32[768,768]{1,0:T(8,128)}, u32[]{:S(2)}) copy-start(f32[768,768]{1,0:T(8,128)} %get-tuple-element.78) | copy-start | bytes 7077892
  619.0 2.2 copy-start.12
  619.9 2.8 copy-start.1
  (12 other events, 11.2 us)
Sparse Core Ops, SparseCore 0:
  24.6 71.1 all-reduce.7
  113.4 68.5 all-reduce.9
  199.5 68.5 all-reduce.11
  300.1 68.5 all-reduce.13
  374.7 238.3 all-reduce.15
where the time goes:
time: 630 us; the launch traced here: 629 us
  waiting for transfers between devices  456 us (72%)
  matrix products  60.2 us (10%)
  blocking collectives  40.1 us (6%)
  other arithmetic  36.2 us (6%)
  local copies, waits for them, and re-layouts  21.4 us (3%)
  between operations  14.3 us (2%)
    psum x1, waiting for transfers between devices, shards(): lax.psum((mask_embedding_grad, query_weight_grad, query_bias_grad, key_we...  200 us
    psum x1, waiting for transfers between devices, shards(): attended = lax.psum(local_dot(context, out_weight), 'tensor')  71 us
    psum x1, waiting for transfers between devices, shards(): ffn_out = lax.psum(local_dot(activ, down_weight), 'tensor')  68.6 us
    psum x1, waiting for transfers between devices, shards(): grad_one = grad_h2 + lax.psum(dot_trans(grad_pre, up_weight), 'tensor')  60.5 us
    psum x1, waiting for transfers between devices, shards(): grad_in = grad_h1 + lax.psum(input_terms, 'tensor')  56.1 us
    psum x1, blocking collectives, shards(): lax.psum((mask_embedding_grad, query_weight_grad, query_bias_grad, key_we...  40.1 us
    unnamed x116, local copies, waits for them, and re-layouts  21.3 us
    dot_general x6, matrix products, local_dot(): return jnp.dot(left, right, preferred_element_type=jnp.float32)  16.7 us
  transfers between devices with their start and end apart: 5, of which 5 were waited for; matrix products, arithmetic and copies ran while one was open for 4% of the time, Pallas kernels for 0%

commit v1 on v0

v1 whole, which is shorter than its diff:
```python
import math

import jax
import jax.numpy as jnp
from jax import lax
from jax.sharding import PartitionSpec as P

HEAD = 64
AXES = ("dp", "tensor")
STEPS = 2


def local_dot(left, right):
    return jnp.dot(left, right, preferred_element_type=jnp.float32)


def dot_rows(left, right):
    return lax.dot_general(
        left, right, (((0,), (0,)), ((), ())), preferred_element_type=jnp.float32
    )


def dot_trans(left, right):
    return lax.dot_general(
        left, right, (((1,), (1,)), ((), ())), preferred_element_type=jnp.float32
    )


def normalize(values):
    centered = values - jnp.mean(values, -1, keepdims=True)
    inverse = lax.rsqrt(jnp.mean(centered * centered, -1, keepdims=True) + 1e-05)
    return (centered * inverse, inverse)


def norm_backward(grad_normed, normed, inverse):
    return inverse * (
        grad_normed
        - jnp.mean(grad_normed, -1, keepdims=True)
        - normed * jnp.mean(grad_normed * normed, -1, keepdims=True)
    )


class Swaps:
    def __init__(self, mesh):
        self.dp = mesh.shape["dp"]
        self.tensor = mesh.shape["tensor"]
        index = lax.axis_index("dp")
        self.masks = [1 << bit for bit in range(self.dp.bit_length() - 1)]
        self.coords = [(index >> bit) & 1 for bit in range(len(self.masks))]
        if len(self.masks) >= 3:
            self.masks[2] = 6
            self.coords[1] = self.coords[1] ^ self.coords[2]
        self.core = lax.axis_index("tensor") % 2

    def move(self, value, target):
        pairs = []
        for row in range(self.dp):
            for column in range(self.tensor):
                to_row, to_column = target(row, column)
                pairs.append((row * self.tensor + column, to_row * self.tensor + to_column))
        return lax.ppermute(value, AXES, pairs)

    def over_core(self, value):
        return self.move(value, lambda row, column: (row, column ^ 1))

    def over_chip(self, value):
        return self.move(value, lambda row, column: (row, column ^ 2))

    def over_dp(self, value, even, odd):
        masks = self.masks
        return self.move(
            value, lambda row, column: (row ^ masks[odd if column % 2 else even], column)
        )

    def plan(self):
        steps = list(range(len(self.masks)))
        result = []
        for even, odd in zip(steps, steps[-1:] + steps[:-1]):
            coord = jnp.where(self.core == 0, self.coords[even], self.coords[odd])
            result.append((even, odd, coord))
        return result


class Order:
    def __init__(self):
        self.last = ()

    def begin(self, *arrays):
        arrays, _ = lax.optimization_barrier((arrays, self.last))
        return arrays[0] if len(arrays) == 1 else arrays

    def end(self, *arrays):
        self.last = arrays
        return arrays[0] if len(arrays) == 1 else arrays


class Total:
    def __init__(self, swaps, order, value):
        self.swaps, self.order, self.plan = swaps, order, swaps.plan()
        self.queue = [self.first] + [self.halve] * (len(self.plan) - 2)
        self.queue += [self.exchange, self.settle] + [self.double] * (len(self.plan) - 1)
        self.keep, self.got, self.at = value, None, 0
        self.advance()

    def advance(self, count=1):
        for _ in range(count):
            if self.queue:
                self.queue.pop(0)()

    def send(self, value):
        even, odd, _ = self.plan[self.at]
        self.got = self.swaps.over_dp(value, even, odd)

    def first(self):
        coord = self.plan[0][2]
        rows = self.keep.shape[0] // 2
        value = self.order.begin(self.keep)
        self.send(self.order.end(pick(value, 1 - coord, rows)))
        self.keep = pick(value, coord, rows)

    def halve(self):
        self.at += 1
        coord = self.plan[self.at][2]
        rows = self.keep.shape[0] // 2
        keep, got = self.order.begin(self.keep, self.got)
        send = pick(keep, 1 - coord, rows) + pick(got, 1 - coord, rows)
        self.keep = pick(keep, coord, rows) + pick(got, coord, rows)
        self.order.end(send, self.keep)
        self.send(send)

    def exchange(self):
        self.at += 1
        keep, got = self.order.begin(self.keep, self.got)
        self.keep = self.order.end(keep + got)
        self.send(self.keep)

    def settle(self):
        keep, got = self.order.begin(self.keep, self.got)
        self.keep = self.order.end(keep + got)
        self.at -= 1
        self.send(self.keep)

    def double(self):
        first = self.plan[self.at][2] == 0
        keep, got = self.order.begin(self.keep, self.got)
        self.keep = self.order.end(
            jnp.concatenate([jnp.where(first, keep, got), jnp.where(first, got, keep)], 0)
        )
        self.at -= 1
        if self.at >= 0:
            self.send(self.keep)

    def finish(self):
        self.advance(len(self.queue))
        return self.keep


def pick(block, part, rows):
    return lax.dynamic_slice_in_dim(block, part * rows, rows, 0)


def widen(array):
    return array.astype(jnp.float32) * 2.0


def narrow(array):
    return (array * 0.5).astype(jnp.bfloat16)


def shards(
    mesh,
    frames,
    frame_mask,
    mask_embedding,
    query_weight,
    query_bias,
    key_weight,
    value_weight,
    value_bias,
    out_weight,
    out_bias,
    norm1_gain,
    norm1_shift,
    up_weight,
    up_bias,
    down_weight,
    down_bias,
    norm2_gain,
    norm2_shift,
    cotangent,
):
    swaps = Swaps(mesh)
    order = Order()
    clip_count, length, model_width = frames.shape
    token_rows = clip_count * length
    local_width = query_weight.shape[1]
    heads_here = local_width // HEAD
    score_scale = 1.0 / math.sqrt(HEAD)
    head_shape = (clip_count, length, heads_here, HEAD)
    own_rows = token_rows // 2
    step_rows = own_rows // STEPS
    core = swaps.core
    tensor_index = lax.axis_index("tensor")

    def own_first(array):
        view = array.reshape((2, own_rows) + array.shape[1:])
        return jnp.where(core == 0, view, view[::-1]).reshape(array.shape)

    def step(array, k):
        return array[k * step_rows : (k + 1) * step_rows]

    out_all = lax.all_gather(widen(out_weight), "tensor", tiled=True)
    up_pair = swaps.over_core(widen(up_weight))
    down_pair = swaps.over_core(widen(down_weight))
    up_bias_pair = swaps.over_core(up_bias.reshape(1, -1))[0]

    masked_rows = own_first(frame_mask.reshape(token_rows, 1)).astype(jnp.float32)
    masked_in = (
        own_first(frames.reshape(token_rows, model_width)).astype(jnp.float32)
        * (1.0 - masked_rows)
        + masked_rows * mask_embedding
    )
    grad_out = pick(cotangent.reshape(token_rows, model_width), core, own_rows).astype(jnp.float32)
    masked_low = masked_in.astype(jnp.bfloat16)
    query = (local_dot(masked_low, query_weight) + query_bias).astype(jnp.bfloat16)
    keys = local_dot(masked_low, key_weight).astype(jnp.bfloat16)
    values = (local_dot(masked_low, value_weight) + value_bias).astype(jnp.bfloat16)
    query_heads = query.reshape(head_shape)
    key_heads = keys.reshape(head_shape)
    value_heads = values.reshape(head_shape)
    scores = (
        jnp.einsum("cqhd,ckhd->chqk", query_heads, key_heads, preferred_element_type=jnp.float32)
        * score_scale
    )
    row_max = jnp.max(scores, -1, keepdims=True)
    expo = jnp.exp(scores - row_max)
    totals = jnp.sum(expo, -1, keepdims=True)
    log_sum = row_max + jnp.log(totals)
    attn_low = (expo / totals).astype(jnp.bfloat16)
    context = jnp.einsum(
        "chqk,ckhd->cqhd", attn_low, value_heads, preferred_element_type=jnp.float32
    )
    context = context.reshape(token_rows, local_width).astype(jnp.bfloat16)

    context_pair = swaps.over_core(widen(context[own_rows:]))
    chip_wide = jnp.concatenate([widen(context[:own_rows]), context_pair], 1)
    other_wide = [swaps.over_chip(step(chip_wide, k)) for k in range(STEPS)]
    context_chip = narrow(order.end(chip_wide))
    out_all = narrow(out_all)
    out_parts = [pick(out_all, tensor_index ^ mask, local_width) for mask in (0, 1, 2, 3)]
    out_chip = jnp.concatenate(out_parts[:2], 0)
    out_other = jnp.concatenate(out_parts[2:], 0)
    up_chip = jnp.concatenate([up_weight, narrow(up_pair)], 1)
    up_bias_chip = jnp.concatenate([up_bias, up_bias_pair])
    down_chip = jnp.concatenate([down_weight, narrow(down_pair)], 0)
    units_here = up_weight.shape[1]

    normed_one, inverse_one, ffn_in, activ, slope = [], [], [], [], []
    hidden_one, ffn_part, ffn_got = [], [], []
    for k in range(STEPS):
        rows, wide = order.begin(step(context_chip, k), other_wide[k])
        attended = local_dot(rows, out_chip) + local_dot(narrow(wide), out_other)
        normed, inverse = normalize(step(masked_in, k) + attended + out_bias)
        hidden = normed * norm1_gain + norm1_shift
        low = hidden.astype(jnp.bfloat16)
        pre_act = local_dot(low, up_chip) + up_bias_chip
        normal_cdf = 0.5 * (1.0 + lax.erf(pre_act / math.sqrt(2.0)))
        normal_pdf = jnp.exp(-0.5 * pre_act * pre_act) / math.sqrt(2.0 * math.pi)
        units = (pre_act * normal_cdf).astype(jnp.bfloat16)
        part = order.end(local_dot(units, down_chip))
        ffn_part.append(part)
        ffn_got.append(swaps.over_chip(part))
        normed_one.append(normed)
        inverse_one.append(inverse)
        hidden_one.append(hidden)
        ffn_in.append(low)
        activ.append(units)
        slope.append(normal_cdf + pre_act * normal_pdf)

    output, grad_h2, grad_h2_low, grad_pre, one_part, one_got = [], [], [], [], [], []
    gain_two, shift_two, bias_down, bias_up = [], [], [], []
    for k in range(STEPS):
        part, got = order.begin(ffn_part[k], ffn_got[k])
        normed, inverse = normalize(hidden_one[k] + (part + got) + down_bias)
        output.append(normed)
        grad = step(grad_out, k)
        gain_two.append(jnp.sum(grad * normed, 0))
        shift_two.append(jnp.sum(grad, 0))
        grad_two = norm_backward(grad * norm2_gain, normed, inverse)
        bias_down.append(jnp.sum(grad_two, 0))
        low = grad_two.astype(jnp.bfloat16)
        units = (dot_trans(low, down_chip) * slope[k]).astype(jnp.bfloat16)
        bias_up.append(jnp.sum(units.astype(jnp.float32), 0))
        part = order.end(dot_trans(units, up_chip))
        one_part.append(part)
        one_got.append(swaps.over_chip(part))
        grad_h2.append(grad_two)
        grad_h2_low.append(low)
        grad_pre.append(units)

    activ = jnp.concatenate(activ, 0)
    grad_h2_low = jnp.concatenate(grad_h2_low, 0)
    activ, grad_h2_low = order.begin(activ, grad_h2_low)
    down_send = order.end(dot_rows(activ[:, units_here:], grad_h2_low))
    down_got = swaps.over_core(down_send)
    activ, grad_h2_low = order.begin(activ, grad_h2_low)
    down_keep = order.end(dot_rows(activ[:, :units_here], grad_h2_low))
    ffn_in = jnp.concatenate(ffn_in, 0)
    grad_pre = jnp.concatenate(grad_pre, 0)
    ffn_in, grad_pre = order.begin(ffn_in, grad_pre)
    up_send = order.end(dot_rows(ffn_in, grad_pre[:, units_here:]))
    up_got = swaps.over_core(up_send)
    down_keep, down_got = order.begin(down_keep, down_got)
    down_total = Total(swaps, order, order.end(down_keep + down_got))
    ffn_in, grad_pre = order.begin(ffn_in, grad_pre)
    up_keep = order.end(dot_rows(ffn_in, grad_pre[:, :units_here]))
    up_keep, up_got = order.begin(up_keep, up_got)
    up_total = Total(swaps, order, order.end(up_keep + up_got))

    gain_one, shift_one, bias_out, grad_h1, grad_h1_low, wide_context = [], [], [], [], [], []
    context_grads = []
    for k in range(STEPS):
        part, got = order.begin(one_part[k], one_got[k])
        grad_one = grad_h2[k] + (part + got)
        gain_one.append(jnp.sum(grad_one * normed_one[k], 0))
        shift_one.append(jnp.sum(grad_one, 0))
        grad = norm_backward(grad_one * norm1_gain, normed_one[k], inverse_one[k])
        bias_out.append(jnp.sum(grad, 0))
        low = grad.astype(jnp.bfloat16)
        grad_h1.append(grad)
        grad_h1_low.append(low)
        wide_context.append(widen(dot_trans(low, out_parts[1]).astype(jnp.bfloat16)))
        context_grads.append(dot_trans(low, out_parts[0]).astype(jnp.bfloat16))
        order.end(wide_context[-1], context_grads[-1])
        if k == STEPS // 2 - 1:
            down_total.advance()
    got = swaps.over_core(jnp.concatenate(wide_context, 0))
    down_total.advance()
    up_total.advance()
    grad_context = jnp.concatenate(context_grads + [narrow(got)], 0).reshape(head_shape)
    grad_h1_low = jnp.concatenate(grad_h1_low, 0)

    grad_context, scale_sum = order.begin(grad_context, log_sum)
    scores_again = (
        jnp.einsum("cqhd,ckhd->chqk", query_heads, key_heads, preferred_element_type=jnp.float32)
        * score_scale
    )
    attn_again = jnp.exp(scores_again - scale_sum)
    attn_again_low = attn_again.astype(jnp.bfloat16)
    grad_values = jnp.einsum(
        "chqk,cqhd->ckhd", attn_again_low, grad_context, preferred_element_type=jnp.float32
    )
    grad_values = grad_values.astype(jnp.bfloat16).reshape(token_rows, local_width)
    grad_attn = jnp.einsum(
        "cqhd,ckhd->chqk", grad_context, value_heads, preferred_element_type=jnp.float32
    )
    grad_scores = (
        attn_again * (grad_attn - jnp.sum(attn_again * grad_attn, -1, keepdims=True))
    ).astype(jnp.bfloat16)
    order.end(grad_scores, grad_values)
    down_total.advance()
    up_total.advance()
    grad_scores = order.begin(grad_scores)
    grad_query = (
        jnp.einsum("chqk,ckhd->cqhd", grad_scores, key_heads, preferred_element_type=jnp.float32)
        * score_scale
    )
    grad_query = grad_query.astype(jnp.bfloat16).reshape(token_rows, local_width)
    grad_keys = (
        jnp.einsum("chqk,cqhd->ckhd", grad_scores, query_heads, preferred_element_type=jnp.float32)
        * score_scale
    )
    grad_keys = grad_keys.astype(jnp.bfloat16).reshape(token_rows, local_width)
    three = order.end(jnp.concatenate([grad_query, grad_keys, grad_values], 1))
    attn_weight = jnp.concatenate([query_weight, key_weight, value_weight], 1)

    three = order.begin(three)
    terms_send = order.end(dot_trans(three[own_rows:], attn_weight))
    terms_got = swaps.over_core(terms_send)
    three = order.begin(three)
    terms_keep = order.end(dot_trans(three[:own_rows], attn_weight))
    chip_terms, chip_got = [], []
    for k in range(2):
        rows = own_rows // 2
        part, got = order.begin(
            terms_keep[k * rows : (k + 1) * rows], terms_got[k * rows : (k + 1) * rows]
        )
        chip_terms.append(order.end(part + got))
        chip_got.append(swaps.over_chip(chip_terms[-1]))
    three = order.begin(three)
    attn_total = Total(swaps, order, order.end(dot_rows(masked_low, three)))
    grad_h1_low, context_chip = order.begin(grad_h1_low, context_chip)
    out_send = order.end(dot_rows(context_chip[:, local_width:], grad_h1_low))
    out_got = swaps.over_core(out_send)
    out_keep = order.end(dot_rows(context_chip[:, :local_width], grad_h1_low))
    down_total.advance()
    up_total.advance()
    out_keep, out_got = order.begin(out_keep, out_got)
    out_total = Total(swaps, order, order.end(out_keep + out_got))
    attn_total.advance()
    down_total.advance()
    up_total.advance()

    frames_part, mask_sums = [], []
    unmasked = 1.0 - masked_rows
    for k in range(2):
        rows = own_rows // 2
        part, got = order.begin(chip_terms[k], chip_got[k])
        grad_in = jnp.concatenate(grad_h1, 0)[k * rows : (k + 1) * rows] + (part + got)
        mask_sums.append(jnp.sum(grad_in * masked_rows[k * rows : (k + 1) * rows], 0))
        frames_part.append(order.end(grad_in))
        down_total.advance()
        up_total.advance()
        attn_total.advance()
        out_total.advance()
    frames_part = jnp.concatenate(frames_part, 0)
    frames_got = swaps.over_core(frames_part)
    output = jnp.concatenate(output, 0)
    output_got = swaps.over_core(output)

    shared = (
        sum(mask_sums),
        sum(bias_out),
        sum(gain_one),
        sum(shift_one),
        sum(bias_down),
        sum(gain_two),
        sum(shift_two),
    )
    own_bias_up = sum(bias_up)
    pair = jnp.concatenate(shared + (own_bias_up[units_here:],))[None]
    mine = jnp.concatenate(shared + (own_bias_up[:units_here],))[None]
    packed = mine + swaps.over_core(pair)
    packed = jnp.concatenate(
        [
            packed,
            jnp.sum(grad_query.astype(jnp.float32), 0)[None],
            jnp.sum(grad_values.astype(jnp.float32), 0)[None],
        ],
        1,
    )
    for link in range(len(swaps.masks)):
        packed = packed + swaps.over_dp(packed, link, link)
    pieces = []
    start = 0
    for width in [model_width] * 7 + [units_here] + [local_width] * 2:
        pieces.append(packed[0, start : start + width])
        start += width
    (
        mask_embedding_grad,
        out_bias_grad,
        norm1_gain_grad,
        norm1_shift_grad,
        down_bias_grad,
        norm2_gain_grad,
        norm2_shift_grad,
        up_bias_grad,
        query_bias_grad,
        value_bias_grad,
    ) = pieces
    down_weight_grad = down_total.finish()
    up_weight_grad = up_total.finish()
    for _ in range(4):
        attn_total.advance()
        out_total.advance()
    attn_weight_grad = attn_total.finish()
    out_weight_grad = out_total.finish()
    query_weight_grad = attn_weight_grad[:, :local_width]
    key_weight_grad = attn_weight_grad[:, local_width : 2 * local_width]
    value_weight_grad = attn_weight_grad[:, 2 * local_width :]

    def in_place(own, got):
        whole = jnp.stack([jnp.where(core == 0, own, got), jnp.where(core == 0, got, own)])
        return whole.reshape(token_rows, model_width)

    frames_grad = in_place(frames_part, frames_got) * (
        1.0 - frame_mask.reshape(token_rows, 1).astype(jnp.float32)
    )
    output = in_place(output, output_got) * norm2_gain + norm2_shift
    return (
        output.astype(jnp.bfloat16).reshape(frames.shape),
        frames_grad.astype(jnp.bfloat16).reshape(frames.shape),
        mask_embedding_grad,
        query_weight_grad,
        query_bias_grad,
        key_weight_grad,
        value_weight_grad,
        value_bias_grad,
        out_weight_grad,
        out_bias_grad,
        norm1_gain_grad,
        norm1_shift_grad,
        up_weight_grad,
        up_bias_grad,
        down_weight_grad,
        down_bias_grad,
        norm2_gain_grad,
        norm2_shift_grad,
    )


def solution(mesh):
    rows, columns, whole, vector = P("dp"), P(None, "tensor"), P(), P("tensor")
    return jax.shard_map(
        lambda *arrays: shards(mesh, *arrays),
        mesh=mesh,
        in_specs=(
            P("dp", None, None),
            P("dp", None),
            whole,
            columns,
            vector,
            columns,
            columns,
            vector,
            P("tensor", None),
            whole,
            whole,
            whole,
            columns,
            vector,
            P("tensor", None),
            whole,
            whole,
            whole,
            P("dp", None, None),
        ),
        out_specs=(
            P("dp", None, None),
            P("dp", None, None),
            whole,
            columns,
            vector,
            columns,
            columns,
            vector,
            P("tensor", None),
            whole,
            whole,
            whole,
            columns,
            vector,
            P("tensor", None),
            whole,
            whole,
            whole,
        ),
        check_vma=False,
    )
```

time: 630 us -> 426 us (0.68)
  the two profiles are of different devices: /device:TPU:0 before, /device:TPU:9 now
where the time goes in v1:
time: 426 us; the launch traced here: 419 us
  waiting for transfers between devices  188 us (44%)
  other arithmetic  75.8 us (18%)
  matrix products  74.3 us (17%)
  local copies, waits for them, and re-layouts  32.6 us (8%)
  starting transfers between devices  32.2 us (8%)
  between operations  16 us (4%)
    ppermute x43, waiting for transfers between devices, move(): return lax.ppermute(value, AXES, pairs)  188 us
    ppermute x43, starting transfers between devices, move(): return lax.ppermute(value, AXES, pairs)  32.2 us
    sub x1, matrix products, shards(): grad_attn - jnp.sum(attn_again * grad_attn, -1, keepdims=True)  17.5 us
    unnamed x187, local copies, waits for them, and re-layouts  16.7 us
    dot_general x10, matrix products, dot_trans(): lax.dot_general(left, right, (((1,), (1,)), ((), ())), preferred_element_...  15.2 us
    dot_general x7, matrix products, dot_rows(): lax.dot_general(left, right, (((0,), (0,)), ((), ())), preferred_element_...  10.8 us
  transfers between devices with their start and end apart: 44, of which 17 were waited for; matrix products, arithmetic and copies ran while one was open for 33% of the time, Pallas kernels for 0%

profile of v1, /device:TPU:9, one launch (start us, length us, event | category | flops | bytes accessed | tf_op | source)
XLA Modules:
  0.0 418.7 jit_solution(6033548837644019121)
XLA Ops:
  7.2 1.9 convert_multiply_fusion.3
  15.2 2.2 fusion.15
  20.4 1.9 multiply_reduce_fusion.1
  22.2 2.1 fusion.2
  24.3 2.5 copy-done
  26.8 2.8 fusion.58
  35.5 7.2 %collective-permute-done.1 = f32[256,384]{0,1:T(8,128)S(1)} collective-permute-done((f32[256,384]{0,1:T(8,128)S(1)}, f32[256,384]{0,1:T(8,128)S(1)}, u32[]{:S(2)}, u32[]{:S(2)}) %collective-permute-start.1) | collective-permute-done | bytes 393248 | tf_op jit(solution)/shard_map/ppermute | solution.py:61
  42.8 2.9 multiply_convert_fusion.2
  45.6 2.9 multiply_convert_fusion.1
  62.5 11.2 %collective-permute-done.5 = f32[256,768]{1,0:T(8,128)S(1)} collective-permute-done((f32[256,768]{1,0:T(8,128)S(1)}, f32[256,768]{1,0:T(8,128)S(1)}, u32[]{:S(2)}, u32[]{:S(2)}) %collective-permute-start.5) | collective-permute-done | bytes 786464 | tf_op jit(solution)/shard_map/ppermute | solution.py:61
  76.6 3.4 convert_reduce_fusion.1
  81.7 8.9 %collective-permute-done.7 = f32[256,768]{1,0:T(8,128)S(1)} collective-permute-done((f32[256,768]{1,0:T(8,128)S(1)}, f32[256,768]{1,0:T(8,128)S(1)}, u32[]{:S(2)}, u32[]{:S(2)}) %collective-permute-start.7) | collective-permute-done | bytes 786464 | tf_op jit(solution)/shard_map/ppermute | solution.py:61
  93.8 3.3 convert_reduce_fusion
  98.9 2.2 fusion.71
  101.1 3.0 collective-permute-start.10
  104.1 2.2 fusion.69
  106.4 2.2 fusion.67
  111.2 2.7 add.395
  116.4 2.0 add.397
  120.0 7.5 %collective-permute-done.9 = f32[256,768]{1,0:T(8,128)S(1)} collective-permute-done((f32[256,768]{1,0:T(8,128)}, f32[256,768]{1,0:T(8,128)S(1)}, u32[]{:S(2)}, u32[]{:S(2)}) %collective-permute-start.9) | collective-permute-done | bytes 786464 | tf_op jit(solution)/shard_map/ppermute | solution.py:61
  131.0 23.5 %collective-permute-done.13 = f32[384,768]{1,0:T(8,128)S(1)} collective-permute-done((f32[384,768]{1,0:T(8,128)S(1)}, f32[384,768]{1,0:T(8,128)S(1)}, u32[]{:S(2)}, u32[]{:S(2)}) %collective-permute-start.13) | collective-permute-done | bytes 1179680 | tf_op jit(solution)/shard_map/ppermute | solution.py:61
  160.9 7.4 %collective-permute-done.16 = f32[192,768]{1,0:T(8,128)S(1)} collective-permute-done((f32[192,768]{1,0:T(8,128)S(1)}, f32[192,768]{1,0:T(8,128)S(1)}, u32[]{:S(2)}, u32[]{:S(2)}) %collective-permute-start.16) | collective-permute-done | bytes 589856 | tf_op jit(solution)/shard_map/ppermute | solution.py:61
  171.6 6.4 %fusion.87 = f32[3,1024,1024]{1,2,0:T(8,128)} fusion(bf16[1024,3,64]{0,2,1:T(8,128)(2,1)S(1)} %bitcast.181, bf16[1,1024,3,64]{1,3,2,0:T(8,128)(2,1)S(1)} %bitcast.166), kind=kOutput, calls=%fused_computation.196 | convolution fusion | flops 402653184 | bytes 13369344 | tf_op jit(solution)/shard_map/cqhd,ckhd->chqk/dot_general | solution.py:354
  178.0 17.5 %fusion.21 = bf16[1,3,1024,1024]{2,3,1,0:T(8,128)(2,1)} fusion(f32[3,1024,1024]{1,2,0:T(8,128)} %fusion.87, f32[3,1024]{1,0:T(4,128)S(1)} %bitcast.183, bf16[1024,3,64]{0,2,1:T(8,128)(2,1)S(1)} %bitcast.171, bf16[1024,3,64]{0,2,1:T(8,128)(2,1)} %bitcast.174), kind=kOutput, calls=%fused_computation.39 | convolution fusion | flops 830476288 | bytes 19673088 | tf_op jit(solution)/shard_map/sub | solution.py:358
  195.5 7.7 %convert_reduce_fusion.2 = (f32[3,64]{1,0:T(4,128)}, bf16[3,64,1024]{2,1,0:T(8,128)(2,1)S(1)}) fusion(f32[3,1024,1024]{1,2,0:T(8,128)} %copy-done, f32[3,1024]{1,0:T(4,128)S(1)} %bitcast.184, bf16[1,1024,3,64]{1,3,2,0:T(8,128)(2,1)S(1)} %bitcast.167), kind=kOutput, calls=%fused_computation.120 | convolution fusion | flops 412680000 | bytes 13382400 | tf_op jit(solution)/shard_map/chqk,cqhd->ckhd/dot_general | solution.py:350
  203.2 2.2 add.412
  205.4 2.0 add.413
  207.4 2.0 fusion.46
  209.4 1.9 convert_reduce_fusion.3
  212.4 2.0 fusion.80
  217.5 2.0 fusion.82
  228.4 2.0 collective-permute-start.21
  232.6 24.7 %collective-permute-done.21 = f32[192,768]{1,0:T(8,128)} collective-permute-done((f32[192,768]{1,0:T(8,128)S(1)}, f32[192,768]{1,0:T(8,128)}, u32[]{:S(2)}, u32[]{:S(2)}) %collective-permute-start.21) | collective-permute-done | bytes 589856 | tf_op jit(solution)/shard_map/ppermute | solution.py:61
  261.5 42.5 %collective-permute-done.25 = f32[384,576]{0,1:T(8,128)} collective-permute-done((f32[384,576]{0,1:T(8,128)}, f32[384,576]{0,1:T(8,128)}, u32[]{:S(2)}, u32[]{:S(2)}) %collective-permute-start.25) | collective-permute-done | bytes 884768 | tf_op jit(solution)/shard_map/ppermute | solution.py:61
  304.0 3.1 dynamic-slice_add_fusion.1
  317.4 4.6 %collective-permute-done.20 = f32[256,768]{1,0:T(8,128)} collective-permute-done((f32[256,768]{1,0:T(8,128)}, f32[256,768]{1,0:T(8,128)}, u32[]{:S(2)}, u32[]{:S(2)}) %collective-permute-start.20) | collective-permute-done | bytes 786464 | tf_op jit(solution)/shard_map/ppermute | solution.py:61
  322.0 2.1 multiply_reduce_fusion.5
  324.1 12.2 %collective-permute-done.30 = f32[384,768]{1,0:T(8,128)} collective-permute-done((f32[384,768]{1,0:T(8,128)S(1)}, f32[384,768]{1,0:T(8,128)}, u32[]{:S(2)}, u32[]{:S(2)}) %collective-permute-start.30) | collective-permute-done | bytes 1179680 | tf_op jit(solution)/shard_map/ppermute | solution.py:61
  344.5 10.0 %collective-permute-done.36 = f32[192,576]{1,0:T(8,128)S(1)} collective-permute-done((f32[192,576]{1,0:T(8,128)S(1)}, f32[192,576]{1,0:T(8,128)S(1)}, u32[]{:S(2)}, u32[]{:S(2)}) %collective-permute-start.36) | collective-permute-done | bytes 442400 | tf_op jit(solution)/shard_map/ppermute | solution.py:61
  355.3 2.1 copy.48
  357.4 2.3 add.443
  359.7 2.1 copy.49
  367.0 3.5 collective-permute-done.33
  374.8 2.1 copy.50
  378.9 3.6 collective-permute-done.41
  385.4 15.7 %collective-permute-done.42 = f32[96,768]{1,0:T(8,128)S(1)} collective-permute-done((f32[96,768]{1,0:T(8,128)S(1)}, f32[96,768]{1,0:T(8,128)S(1)}, u32[]{:S(2)}, u32[]{:S(2)}) %collective-permute-start.42) | collective-permute-done | bytes 294944 | tf_op jit(solution)/shard_map/ppermute | solution.py:61
  402.0 2.4 select_bitcast_fusion.1
  407.7 2.6 collective-permute-done.39
  (410 shorter events, 115.9 us)
Async XLA Ops:
  7.2 41.3 %all-gather.2.cloned.1.call-start = ((), (), s32[]{:S(2)}) async-start(), calls=%async_computation | async-start | bytes 2949120 | tf_op jit(solution)/shard_map/all_gather | solution.py:212
  10.8 32.0 %collective-permute-start.2 = (f32[768,768]{1,0:T(8,128)}, f32[768,768]{1,0:T(8,128)}, u32[]{:S(2)}, u32[]{:S(2)}) collective-permute-start(f32[768,768]{1,0:T(8,128)} %convert_multiply_fusion.2), channel_id=1, source_target_pairs={{0,1},{1,0},{2,3},{3,2},{4,5},{5,4},{6,7},{7,6},{8,9},{9,8},{10,11... | collective-permute-start | bytes 7077896 | tf_op jit(solution)/shard_map/ppermute | solution.py:61
  13.0 32.6 %collective-permute-start.4 = (f32[768,768]{1,0:T(8,128)}, f32[768,768]{1,0:T(8,128)}, u32[]{:S(2)}, u32[]{:S(2)}) collective-permute-start(f32[768,768]{1,0:T(8,128)} %convert_multiply_fusion.1), channel_id=1, source_target_pairs={{0,1},{1,0},{2,3},{3,2},{4,5},{5,4},{6,7},{7,6},{8,9},{9,8},{10,11... | collective-permute-start | bytes 7077896 | tf_op jit(solution)/shard_map/ppermute | solution.py:61
  29.8 1.9 collective-permute-start
  30.2 1.4 collective-permute-start.3
  32.5 10.3 %collective-permute-start.1 = (f32[256,384]{0,1:T(8,128)S(1)}, f32[256,384]{0,1:T(8,128)S(1)}, u32[]{:S(2)}, u32[]{:S(2)}) collective-permute-start(f32[256,384]{0,1:T(8,128)S(1)} %get-tuple-element.265), channel_id=1, source_target_pairs={{0,2},{1,3},{2,0},{3,1},{4,6},{5,7},{6,4},{7,5},{8,10},{9,11},{10,... | collective-permute-start | bytes 1179656 | tf_op jit(solution)/shard_map/ppermute | solution.py:61
  33.7 24.2 %collective-permute-start.6 = (f32[256,384]{0,1:T(8,128)}, f32[256,384]{0,1:T(8,128)}, u32[]{:S(2)}, u32[]{:S(2)}) collective-permute-start(f32[256,384]{0,1:T(8,128)} %get-tuple-element.266), channel_id=1, source_target_pairs={{0,2},{1,3},{2,0},{3,1},{4,6},{5,7},{6,4},{7,5},{8,10},{9,11},{10,... | collective-permute-start | bytes 1179656 | tf_op jit(solution)/shard_map/ppermute | solution.py:61
  56.6 17.1 %collective-permute-start.5 = (f32[256,768]{1,0:T(8,128)S(1)}, f32[256,768]{1,0:T(8,128)S(1)}, u32[]{:S(2)}, u32[]{:S(2)}) collective-permute-start(f32[256,768]{1,0:T(8,128)S(1)} %fusion.107), channel_id=1, source_target_pairs={{0,2},{1,3},{2,0},{3,1},{4,6},{5,7},{6,4},{7,5},{8,10},{9,11},{10,... | collective-permute-start | bytes 2359304 | tf_op jit(solution)/shard_map/ppermute | solution.py:61
  62.0 28.6 %collective-permute-start.7 = (f32[256,768]{1,0:T(8,128)S(1)}, f32[256,768]{1,0:T(8,128)S(1)}, u32[]{:S(2)}, u32[]{:S(2)}) collective-permute-start(f32[256,768]{1,0:T(8,128)S(1)} %fusion.106), channel_id=1, source_target_pairs={{0,2},{1,3},{2,0},{3,1},{4,6},{5,7},{6,4},{7,5},{8,10},{9,11},{10,... | collective-permute-start | bytes 2359304 | tf_op jit(solution)/shard_map/ppermute | solution.py:61
  62.3 44.1 %copy-start.17 = (bf16[512,768]{1,0:T(8,128)(2,1)}, bf16[512,768]{1,0:T(8,128)(2,1)S(1)}, u32[]{:S(2)}) copy-start(bf16[512,768]{1,0:T(8,128)(2,1)S(1)} %pad_maximum_fusion.16) | copy-start | bytes 2359300
  62.4 11.9 %copy-start.59 = (f32[768]{0:T(1024)S(1)}, f32[768]{0:T(1024)}, u32[]{:S(2)}) copy-start(f32[768]{0:T(1024)} %param.35) | copy-start | bytes 9220
  101.1 10.1 %collective-permute-start.10 = (f32[768,768]{1,0:T(8,128)}, f32[768,768]{1,0:T(8,128)}, u32[]{:S(2)}, u32[]{:S(2)}) collective-permute-start(f32[768,768]{1,0:T(8,128)} %fusion.71), channel_id=1, source_target_pairs={{0,1},{1,0},{2,3},{3,2},{4,5},{5,4},{6,7},{7,6},{8,9},{9,8},{10,11... | collective-permute-start | bytes 7077896 | tf_op jit(solution)/shard_map/ppermute | solution.py:61
  108.6 7.7 %collective-permute-start.11 = (f32[768,768]{1,0:T(8,128)}, f32[768,768]{1,0:T(8,128)}, u32[]{:S(2)}, u32[]{:S(2)}) collective-permute-start(f32[768,768]{1,0:T(8,128)} %fusion.67), channel_id=1, source_target_pairs={{0,1},{1,0},{2,3},{3,2},{4,5},{5,4},{6,7},{7,6},{8,9},{9,8},{10,11... | collective-permute-start | bytes 7077896 | tf_op jit(solution)/shard_map/ppermute | solution.py:61
  108.6 18.9 %collective-permute-start.9 = (f32[256,768]{1,0:T(8,128)}, f32[256,768]{1,0:T(8,128)S(1)}, u32[]{:S(2)}, u32[]{:S(2)}) collective-permute-start(f32[256,768]{1,0:T(8,128)} %fusion.109), channel_id=1, source_target_pairs={{0,2},{1,3},{2,0},{3,1},{4,6},{5,7},{6,4},{7,5},{8,10},{9,11},{10,... | collective-permute-start | bytes 2359304 | tf_op jit(solution)/shard_map/ppermute | solution.py:61
  110.9 43.7 %collective-permute-start.12 = (f32[256,768]{1,0:T(8,128)}, f32[256,768]{1,0:T(8,128)S(1)}, u32[]{:S(2)}, u32[]{:S(2)}) collective-permute-start(f32[256,768]{1,0:T(8,128)} %fusion.108), channel_id=1, source_target_pairs={{0,2},{1,3},{2,0},{3,1},{4,6},{5,7},{6,4},{7,5},{8,10},{9,11},{10,... | collective-permute-start | bytes 2359304 | tf_op jit(solution)/shard_map/ppermute | solution.py:61
  114.1 40.4 %collective-permute-start.13 = (f32[384,768]{1,0:T(8,128)S(1)}, f32[384,768]{1,0:T(8,128)S(1)}, u32[]{:S(2)}, u32[]{:S(2)}) collective-permute-start(f32[384,768]{1,0:T(8,128)S(1)} %get-tuple-element.238), channel_id=1, source_target_pairs={{0,4},{1,25},{2,6},{3,27},{4,0},{5,29},{6,2},{7,31},{8,12},{9,17},... | collective-permute-start | bytes 3538952 | tf_op jit(solution)/shard_map/ppermute | solution.py:61
  118.5 50.6 %collective-permute-start.15 = (f32[384,768]{1,0:T(8,128)S(1)}, f32[384,768]{1,0:T(8,128)S(1)}, u32[]{:S(2)}, u32[]{:S(2)}) collective-permute-start(f32[384,768]{1,0:T(8,128)S(1)} %get-tuple-element.235), channel_id=1, source_target_pairs={{0,4},{1,25},{2,6},{3,27},{4,0},{5,29},{6,2},{7,31},{8,12},{9,17},... | collective-permute-start | bytes 3538952 | tf_op jit(solution)/shard_map/ppermute | solution.py:61
  158.2 2.6 collective-permute-start.14
  159.2 9.1 %collective-permute-start.16 = (f32[192,768]{1,0:T(8,128)S(1)}, f32[192,768]{1,0:T(8,128)S(1)}, u32[]{:S(2)}, u32[]{:S(2)}) collective-permute-start(f32[192,768]{1,0:T(8,128)S(1)} %get-tuple-element.237), channel_id=1, source_target_pairs={{0,8},{1,5},{2,10},{3,7},{4,12},{5,1},{6,14},{7,3},{8,0},{9,13},{1... | collective-permute-start | bytes 1769480 | tf_op jit(solution)/shard_map/ppermute | solution.py:61
  169.1 34.1 %collective-permute-start.18 = (f32[192,768]{1,0:T(8,128)}, f32[192,768]{1,0:T(8,128)}, u32[]{:S(2)}, u32[]{:S(2)}) collective-permute-start(f32[192,768]{1,0:T(8,128)} %add.409), channel_id=1, source_target_pairs={{0,24},{1,9},{2,26},{3,11},{4,28},{5,13},{6,30},{7,15},{8,16},{9,1... | collective-permute-start | bytes 1769480 | tf_op jit(solution)/shard_map/ppermute | solution.py:61
  170.3 35.1 %collective-permute-start.17 = (f32[192,768]{1,0:T(8,128)}, f32[192,768]{1,0:T(8,128)}, u32[]{:S(2)}, u32[]{:S(2)}) collective-permute-start(f32[192,768]{1,0:T(8,128)} %get-tuple-element.233), channel_id=1, source_target_pairs={{0,8},{1,5},{2,10},{3,7},{4,12},{5,1},{6,14},{7,3},{8,0},{9,13},{1... | collective-permute-start | bytes 1769480 | tf_op jit(solution)/shard_map/ppermute | solution.py:61
  195.5 11.8 %copy-start.1 = (bf16[1,3,1024,1024]{2,3,1,0:T(8,128)(2,1)S(1)}, bf16[1,3,1024,1024]{2,3,1,0:T(8,128)(2,1)}, u32[]{:S(2)}) copy-start(bf16[1,3,1024,1024]{2,3,1,0:T(8,128)(2,1)} %fusion.21) | copy-start | bytes 18874372
  214.4 5.2 %collective-permute-start.19 = (f32[512,768]{1,0:T(8,128)}, f32[512,768]{1,0:T(8,128)}, u32[]{:S(2)}, u32[]{:S(2)}) collective-permute-start(f32[512,768]{1,0:T(8,128)} %fusion.80), channel_id=1, source_target_pairs={{0,1},{1,0},{2,3},{3,2},{4,5},{5,4},{6,7},{7,6},{8,9},{9,8},{10,11... | collective-permute-start | bytes 4718600 | tf_op jit(solution)/shard_map/ppermute | solution.py:61
  216.3 10.8 %collective-permute-start.22 = (f32[192,768]{1,0:T(8,128)}, f32[192,768]{1,0:T(8,128)S(1)}, u32[]{:S(2)}, u32[]{:S(2)}) collective-permute-start(f32[192,768]{1,0:T(8,128)} %add.412), channel_id=1, source_target_pairs={{0,8},{1,5},{2,10},{3,7},{4,12},{5,1},{6,14},{7,3},{8,0},{9,13},{1... | collective-permute-start | bytes 1769480 | tf_op jit(solution)/shard_map/ppermute | solution.py:61
  228.3 78.8 %collective-permute-start.24 = (f32[384,768]{1,0:T(8,128)}, f32[384,768]{1,0:T(8,128)}, u32[]{:S(2)}, u32[]{:S(2)}) collective-permute-start(f32[384,768]{1,0:T(8,128)} %pad_maximum_fusion.12), channel_id=1, source_target_pairs={{0,4},{1,25},{2,6},{3,27},{4,0},{5,29},{6,2},{7,31},{8,12},{9,17},... | collective-permute-start | bytes 3538952 | tf_op jit(solution)/shard_map/ppermute | solution.py:61
  228.4 28.9 %collective-permute-start.21 = (f32[192,768]{1,0:T(8,128)S(1)}, f32[192,768]{1,0:T(8,128)}, u32[]{:S(2)}, u32[]{:S(2)}) collective-permute-start(f32[192,768]{1,0:T(8,128)S(1)} %copy-done.28), channel_id=1, source_target_pairs={{0,24},{1,9},{2,26},{3,11},{4,28},{5,13},{6,30},{7,15},{8,16},{9,1... | collective-permute-start | bytes 1769480 | tf_op jit(solution)/shard_map/ppermute | solution.py:61
  230.4 73.5 %collective-permute-start.25 = (f32[384,576]{0,1:T(8,128)}, f32[384,576]{0,1:T(8,128)}, u32[]{:S(2)}, u32[]{:S(2)}) collective-permute-start(f32[384,576]{0,1:T(8,128)} %get-tuple-element.248), channel_id=1, source_target_pairs={{0,4},{1,25},{2,6},{3,27},{4,0},{5,29},{6,2},{7,31},{8,12},{9,17},... | collective-permute-start | bytes 2654216 | tf_op jit(solution)/shard_map/ppermute | solution.py:61
  232.6 26.8 %collective-permute-start.26 = (f32[192,768]{1,0:T(8,128)}, f32[192,768]{1,0:T(8,128)}, u32[]{:S(2)}, u32[]{:S(2)}) collective-permute-start(f32[192,768]{1,0:T(8,128)} %fusion.91), channel_id=1, source_target_pairs={{0,1},{1,0},{2,3},{3,2},{4,5},{5,4},{6,7},{7,6},{8,9},{9,8},{10,11... | collective-permute-start | bytes 1769480 | tf_op jit(solution)/shard_map/ppermute | solution.py:61
  232.6 26.8 %copy-start.30 = (f32[192,768]{1,0:T(8,128)S(1)}, f32[192,768]{1,0:T(8,128)}, u32[]{:S(2)}) copy-start(f32[192,768]{1,0:T(8,128)} %fusion.93) | copy-start | bytes 1769476
  258.4 52.0 %collective-permute-start.23 = (f32[192,768]{1,0:T(8,128)S(1)}, f32[192,768]{1,0:T(8,128)S(1)}, u32[]{:S(2)}, u32[]{:S(2)}) collective-permute-start(f32[192,768]{1,0:T(8,128)S(1)} %add.416), channel_id=1, source_target_pairs={{0,8},{1,5},{2,10},{3,7},{4,12},{5,1},{6,14},{7,3},{8,0},{9,13},{1... | collective-permute-start | bytes 1769480 | tf_op jit(solution)/shard_map/ppermute | solution.py:61
  310.6 25.8 %collective-permute-start.30 = (f32[384,768]{1,0:T(8,128)S(1)}, f32[384,768]{1,0:T(8,128)}, u32[]{:S(2)}, u32[]{:S(2)}) collective-permute-start(f32[384,768]{1,0:T(8,128)S(1)} %pad_maximum_fusion.13), channel_id=1, source_target_pairs={{0,4},{1,25},{2,6},{3,27},{4,0},{5,29},{6,2},{7,31},{8,12},{9,17},... | collective-permute-start | bytes 3538952 | tf_op jit(solution)/shard_map/ppermute | solution.py:61
  310.8 11.2 %collective-permute-start.20 = (f32[256,768]{1,0:T(8,128)}, f32[256,768]{1,0:T(8,128)}, u32[]{:S(2)}, u32[]{:S(2)}) collective-permute-start(f32[256,768]{1,0:T(8,128)} %add.414), channel_id=1, source_target_pairs={{0,2},{1,3},{2,0},{3,1},{4,6},{5,7},{6,4},{7,5},{8,10},{9,11},{10,... | collective-permute-start | bytes 2359304 | tf_op jit(solution)/shard_map/ppermute | solution.py:61
  313.3 28.9 %collective-permute-start.27 = (f32[256,768]{1,0:T(8,128)}, f32[256,768]{1,0:T(8,128)}, u32[]{:S(2)}, u32[]{:S(2)}) collective-permute-start(f32[256,768]{1,0:T(8,128)} %add.415), channel_id=1, source_target_pairs={{0,2},{1,3},{2,0},{3,1},{4,6},{5,7},{6,4},{7,5},{8,10},{9,11},{10,... | collective-permute-start | bytes 2359304 | tf_op jit(solution)/shard_map/ppermute | solution.py:61
  313.6 27.3 %collective-permute-start.28 = (f32[96,768]{1,0:T(8,128)}, f32[96,768]{1,0:T(8,128)}, u32[]{:S(2)}, u32[]{:S(2)}) collective-permute-start(f32[96,768]{1,0:T(8,128)} %get-tuple-element.271), channel_id=1, source_target_pairs={{0,4},{1,25},{2,6},{3,27},{4,0},{5,29},{6,2},{7,31},{8,12},{9,17},... | collective-permute-start | bytes 884744 | tf_op jit(solution)/shard_map/ppermute | solution.py:61
  316.2 23.1 %collective-permute-start.29 = (f32[192,576]{1,0:T(8,128)S(1)}, f32[192,576]{1,0:T(8,128)}, u32[]{:S(2)}, u32[]{:S(2)}) collective-permute-start(f32[192,576]{1,0:T(8,128)S(1)} %copy.45), channel_id=1, source_target_pairs={{0,8},{1,5},{2,10},{3,7},{4,12},{5,1},{6,14},{7,3},{8,0},{9,13},{1... | collective-permute-start | bytes 1327112 | tf_op jit(solution)/shard_map/ppermute | solution.py:61
  342.2 12.3 %collective-permute-start.36 = (f32[192,576]{1,0:T(8,128)S(1)}, f32[192,576]{1,0:T(8,128)S(1)}, u32[]{:S(2)}, u32[]{:S(2)}) collective-permute-start(f32[192,576]{1,0:T(8,128)S(1)} %copy.47), channel_id=1, source_target_pairs={{0,24},{1,9},{2,26},{3,11},{4,28},{5,13},{6,30},{7,15},{8,16},{9,1... | collective-permute-start | bytes 1327112 | tf_op jit(solution)/shard_map/ppermute | solution.py:61
  361.7 13.0 %collective-permute-start.37 = (f32[192,576]{1,0:T(8,128)}, f32[192,576]{1,0:T(8,128)}, u32[]{:S(2)}, u32[]{:S(2)}) collective-permute-start(f32[192,576]{1,0:T(8,128)} %copy.49), channel_id=1, source_target_pairs={{0,8},{1,5},{2,10},{3,7},{4,12},{5,1},{6,14},{7,3},{8,0},{9,13},{1... | collective-permute-start | bytes 1327112 | tf_op jit(solution)/shard_map/ppermute | solution.py:61
  362.4 1.3 collective-permute-start.32
  363.8 6.7 %collective-permute-start.33 = (f32[1,6528]{1,0:T(1,128)S(1)}, f32[1,6528]{1,0:T(1,128)S(1)}, u32[]{:S(2)}, u32[]{:S(2)}) collective-permute-start(f32[1,6528]{1,0:T(1,128)S(1)} %concatenate.107), channel_id=1, source_target_pairs={{0,4},{1,5},{2,6},{3,7},{4,0},{5,1},{6,2},{7,3},{8,12},{9,13},{10,... | collective-permute-start | bytes 78344 | tf_op jit(solution)/shard_map/ppermute | solution.py:61
  365.9 36.1 %collective-permute-start.8 = (f32[512,768]{1,0:T(8,128)}, f32[512,768]{1,0:T(8,128)}, u32[]{:S(2)}, u32[]{:S(2)}) collective-permute-start(f32[512,768]{1,0:T(8,128)} %pad_maximum_fusion.7), channel_id=1, source_target_pairs={{0,1},{1,0},{2,3},{3,2},{4,5},{5,4},{6,7},{7,6},{8,9},{9,8},{10,11... | collective-permute-start | bytes 4718600 | tf_op jit(solution)/shard_map/ppermute | solution.py:61
  366.3 7.4 %collective-permute-start.38 = (f32[48,768]{1,0:T(8,128)S(1)}, f32[48,768]{1,0:T(8,128)S(1)}, u32[]{:S(2)}, u32[]{:S(2)}) collective-permute-start(f32[48,768]{1,0:T(8,128)S(1)} %get-tuple-element.270), channel_id=1, source_target_pairs={{0,8},{1,5},{2,10},{3,7},{4,12},{5,1},{6,14},{7,3},{8,0},{9,13},{1... | collective-permute-start | bytes 442376 | tf_op jit(solution)/shard_map/ppermute | solution.py:61
  370.5 2.8 collective-permute-start.34
  371.8 30.2 %collective-permute-start.31 = (f32[512,768]{1,0:T(8,128)}, f32[512,768]{1,0:T(8,128)}, u32[]{:S(2)}, u32[]{:S(2)}) collective-permute-start(f32[512,768]{1,0:T(8,128)} %pad_maximum_fusion.10), channel_id=1, source_target_pairs={{0,1},{1,0},{2,3},{3,2},{4,5},{5,4},{6,7},{7,6},{8,9},{9,8},{10,11... | collective-permute-start | bytes 4718600 | tf_op jit(solution)/shard_map/ppermute | solution.py:61
  373.3 5.6 %collective-permute-start.35 = (f32[1,6528]{1,0:T(1,128)S(1)}, f32[1,6528]{1,0:T(1,128)S(1)}, u32[]{:S(2)}, u32[]{:S(2)}) collective-permute-start(f32[1,6528]{1,0:T(1,128)S(1)} %add.441), channel_id=1, source_target_pairs={{0,24},{1,25},{2,26},{3,27},{4,28},{5,29},{6,30},{7,31},{8,16},{9,... | collective-permute-start | bytes 78344 | tf_op jit(solution)/shard_map/ppermute | solution.py:61
  373.8 4.6 %collective-permute-start.40 = (f32[48,768]{1,0:T(8,128)S(1)}, f32[48,768]{1,0:T(8,128)S(1)}, u32[]{:S(2)}, u32[]{:S(2)}) collective-permute-start(f32[48,768]{1,0:T(8,128)S(1)} %add.444), channel_id=1, source_target_pairs={{0,24},{1,9},{2,26},{3,11},{4,28},{5,13},{6,30},{7,15},{8,16},{9,1... | collective-permute-start | bytes 442376 | tf_op jit(solution)/shard_map/ppermute | solution.py:61
  378.4 4.1 collective-permute-start.41
  382.5 18.6 %collective-permute-start.42 = (f32[96,768]{1,0:T(8,128)S(1)}, f32[96,768]{1,0:T(8,128)S(1)}, u32[]{:S(2)}, u32[]{:S(2)}) collective-permute-start(f32[96,768]{1,0:T(8,128)S(1)} %pad_maximum_fusion.28), channel_id=1, source_target_pairs={{0,4},{1,25},{2,6},{3,27},{4,0},{5,29},{6,2},{7,31},{8,12},{9,17},... | collective-permute-start | bytes 884744 | tf_op jit(solution)/shard_map/ppermute | solution.py:61
  385.0 25.3 %collective-permute-start.39 = (f32[384,576]{0,1:T(8,128)S(1)}, f32[384,576]{0,1:T(8,128)S(1)}, u32[]{:S(2)}, u32[]{:S(2)}) collective-permute-start(f32[384,576]{0,1:T(8,128)S(1)} %pad_maximum_fusion.15), channel_id=1, source_target_pairs={{0,4},{1,25},{2,6},{3,27},{4,0},{5,29},{6,2},{7,31},{8,12},{9,17},... | collective-permute-start | bytes 2654216 | tf_op jit(solution)/shard_map/ppermute | solution.py:61
  (87 other events, 233.1 us)
Sparse Core Ops, SparseCore 0:
  10.2 25.6 all-gather.1
